TPU v7x, 256 devices: a whole 4x4x8 slice. The times are simulated.
256 devices in a mesh: chain: 8 (over y, core), sector: 32 (over x, z).
Axes of the slice: x: 4, y: 4, z: 8, core: 2. Of those that a mesh axis runs over, the one named last changes fastest.
Arguments:
- site_tensors: bfloat16 [16, 32, 128, 4, 128], P('chain', 'sector'), may hold values from -0.5 to 0.5
- mpo: bfloat16 [16, 42, 42, 4, 4], P('chain'), may hold values from -0.75 to 0.75
- left_in: bfloat16 [8, 32, 42, 128, 128], P('chain', 'sector'), may hold values from -6 to 6
- right_in: bfloat16 [8, 32, 42, 128, 128], P('chain', 'sector'), may hold values from -6 to 6
- tile_rows: int32 [17, 32], replicated, may hold values from 32 to 128
Outputs:
- left_envs: bfloat16 [16, 32, 42, 128, 128], P('chain', 'sector')
- right_envs: bfloat16 [16, 32, 42, 128, 128], P('chain', 'sector')
- left_edge: bfloat16 [8, 32, 42, 128, 128], P('chain', 'sector')
All inputs are finite; a program needn't handle non-finite values.
Results may differ from a plain program's by a relative error of at most 0.009.
Values may be sent and summed in bfloat16 or wider, within the bound.
A program may use at most 128 MiB of HBM per device.

v0:
```python
import functools

import jax
import jax.numpy as jnp
from jax import lax
from jax.experimental import pallas as pl
from jax.experimental.pallas import tpu as pltpu
from jax.sharding import PartitionSpec as P

groups = ((0, 1), (1, 3), (3, 4))
SLICES = 4
PITCH_EXTRA = 8
ROWS = 8


def stage_one(width, tile, padded, pitch, src, lhs, mid):
    count = lhs.shape[0] // tile

    def pair(i, carry):
        rhs = jnp.concatenate([src[2 * i], src[2 * i + 1]], axis=1)
        prod = jnp.dot(lhs, rhs, preferred_element_type=jnp.float32)
        for s in range(count):
            for j in range(2):
                row = pl.multiple_of((s * padded + 2 * i + j) * pitch, 8)
                mid[pl.ds(row, tile), :] = prod[
                    s * tile : (s + 1) * tile, j * tile : (j + 1) * tile
                ]
        return carry

    lax.fori_loop(0, width // 2, pair, 0)


def stage_two(tile, padded, pitch, start, rows, mid, mpo_part, fin, out, add):
    count = fin.shape[0] // tile

    def block(i, carry):
        base = start + i * ROWS
        left = []
        for j in range(0, ROWS, 2):
            both = [
                mid[pl.ds(base + j + k, count * padded, stride=pitch), :].astype(
                    jnp.bfloat16
                )
                for k in range(2)
            ]
            inner = jnp.dot(
                mpo_part,
                jnp.concatenate(both, axis=1),
                preferred_element_type=jnp.float32,
            ).astype(jnp.bfloat16)
            for k in range(2):
                left.append(
                    jnp.concatenate(
                        [
                            inner[
                                t * padded : (t + 1) * padded,
                                k * tile : (k + 1) * tile,
                            ]
                            for t in range(count)
                        ],
                        axis=1,
                    )
                )
        prod = jnp.dot(
            jnp.concatenate(left, axis=0), fin, preferred_element_type=jnp.float32
        )
        for j in range(ROWS):
            spot = pl.ds(base + j, padded, stride=pitch)
            value = prod[j * padded : (j + 1) * padded]
            if add:
                value = value + out[spot, :]
            out[spot, :] = value
        return carry

    lax.fori_loop(0, rows // ROWS, block, 0)


def emit(width, pitch, start, rows, acc, other, dst):
    def one(w, carry):
        value = acc[pl.ds(pl.multiple_of(w * pitch + start, 8), rows), :]
        if other is not None:
            value = value + other[w, start : start + rows, :].astype(jnp.float32)
        dst[w, start : start + rows, :] = value.astype(jnp.bfloat16)
        return carry

    lax.fori_loop(0, width, one, 0)


def kernel(
    sizes,
    lin, rin, am, at, ml0, ml1, ml2, mr0, mr1, mr2,
    left_out, right_out, edge_out,
    r_one, r_two, p_send, p_recv, s_send, s_recv,
    mid, acc_one, acc_zero, acc_right,
    send_sem, recv_sem,
):
    chain_count, sector_count, sites, width, tile, padded, pitch = sizes
    chain = lax.axis_index("chain")
    sector = lax.axis_index("sector")
    up = lax.rem(sector + 1, sector_count)
    down = lax.rem(sector + sector_count - 1, sector_count)
    after = lax.rem(chain + 1, chain_count)
    before = lax.rem(chain + chain_count - 1, chain_count)
    rows = tile // SLICES
    ml = (ml0, ml1, ml2)
    mr = (mr0, mr1, mr2)

    barrier = pltpu.get_barrier_semaphore()
    for there in ({"sector": up}, {"sector": down}, {"chain": after}, {"chain": before}):
        pl.semaphore_signal(barrier, inc=1, device_id=there)
    pl.semaphore_wait(barrier, 4)

    def piece(src, dst, stream, c, there):
        cut = (slice(None), pl.ds(c * rows, rows), slice(None))
        return pltpu.make_async_remote_copy(
            src_ref=src.at[cut],
            dst_ref=dst.at[cut],
            send_sem=send_sem.at[stream, c],
            recv_sem=recv_sem.at[stream, c],
            device_id=there,
            device_id_type=pl.DeviceIdType.MESH,
        )

    def lhs_of(mats, site, n):
        lo, hi = groups[n]
        return mats[site, lo:hi].reshape((hi - lo) * tile, tile)

    one = functools.partial(stage_one, width, tile, padded, pitch)
    two = functools.partial(stage_two, tile, padded, pitch)
    out = functools.partial(emit, width, pitch)

    def left_pass(src, site, n, acc):
        one(src, lhs_of(at, site, n), mid)
        two(0, tile, mid, ml[n][site], lhs_of(am, site, n), acc, False)

    def right_pass(src, site, n, add):
        one(src, lhs_of(am, site, n), mid)
        two(0, tile, mid, mr[n][site], lhs_of(at, site, n), acc_right, add)

    copies = []
    zero = jnp.zeros((tile, tile), jnp.float32)
    for s in range(2):
        for w in range(width, padded):
            mid[pl.ds((s * padded + w) * pitch, tile), :] = zero

    left_src = lin
    right_src = rin
    for c in range(SLICES):
        copies.append(piece(rin, r_one.at[0], 0, c, {"sector": down}))
        copies[-1].start()
    own = copies[-SLICES:]
    for step in range(sites):
        base = step * 4
        lsite, rsite = step, sites - 1 - step
        one(left_src, lhs_of(at, lsite, 2), mid)
        firsts = []
        for c in range(SLICES):
            two(c * rows, rows, mid, ml[2][lsite], lhs_of(am, lsite, 2), acc_one, False)
            out(c * rows, rows, acc_one, None, p_send.at[step])
            firsts.append(
                piece(p_send.at[step], p_recv.at[step], base + 1, c, {"sector": up})
            )
            firsts[-1].start()
        if step > 0:
            one(r_two.at[step - 1], lhs_of(am, rsite + 1, 2), mid)
            own = []
            for c in range(SLICES):
                two(
                    c * rows, rows, mid, mr[2][rsite + 1], lhs_of(at, rsite + 1, 2),
                    acc_right, True,
                )
                out(c * rows, rows, acc_right, None, right_out.at[rsite + 1])
                own.append(
                    piece(
                        right_out.at[rsite + 1], r_one.at[step], base, c,
                        {"sector": down},
                    )
                )
                own[-1].start()
            copies += own
            right_src = right_out.at[rsite + 1]
        left_pass(left_src, lsite, 1, acc_one)
        right_pass(right_src, rsite, 0, False)
        seconds, relays = [], []
        for c in range(SLICES):
            firsts[c].wait_recv()
            out(c * rows, rows, acc_one, p_recv.at[step], s_send.at[step])
            seconds.append(
                piece(s_send.at[step], s_recv.at[step], base + 2, c, {"sector": up})
            )
            seconds[-1].start()
            own[c].wait_recv()
            relays.append(
                piece(r_one.at[step], r_two.at[step], base + 3, c, {"sector": down})
            )
            relays[-1].start()
        left_pass(left_src, lsite, 0, acc_zero)
        right_pass(r_one.at[step], rsite, 1, True)
        last = step == sites - 1
        for c in range(SLICES):
            seconds[c].wait_recv()
            out(c * rows, rows, acc_zero, s_recv.at[step], left_out.at[lsite])
            if last:
                edge = piece(left_out.at[lsite], edge_out, 4 * sites, c, {"chain": after})

                @pl.when(chain < chain_count - 1)
                def _(edge=edge):
                    edge.start()

        left_src = left_out.at[lsite]
        for c in range(SLICES):
            relays[c].wait_recv()
        copies += firsts + seconds + relays
    right_pass(r_two.at[sites - 1], 0, 2, True)
    for c in range(SLICES):
        out(c * rows, rows, acc_right, None, right_out.at[0])

    @pl.when(chain == 0)
    def _():
        def keep(w, carry):
            edge_out[w] = lin[w]
            return carry

        lax.fori_loop(0, width, keep, 0)

    for c in range(SLICES):
        edge = piece(left_out.at[sites - 1], edge_out, 4 * sites, c, {"chain": after})

        @pl.when(chain > 0)
        def _(edge=edge):
            edge.wait_recv()

        @pl.when(chain < chain_count - 1)
        def _(edge=edge):
            edge.wait_send()

    for copy in copies:
        copy.wait_send()


def masked(site_tensors, tile_rows, first, position, count):
    sites, tile, phys = site_tensors.shape[:3]
    ids = lax.iota(jnp.int32, tile)
    padded = jnp.pad(tile_rows, ((0, 0), (0, 2)))
    window = lax.dynamic_slice(padded, (first, position), (sites + 1, 3))
    left = window[:sites, 0]
    right = jnp.stack([window[1:, n] for n in (0, 1, 1, 2)], axis=1)
    keep = (ids[None, :, None, None] < left[:, None, None, None]) & (
        ids[None, None, None, :] < right[:, None, :, None]
    )
    return jnp.where(keep, site_tensors, jnp.zeros((), site_tensors.dtype))


def shards(chain_count, sector_count, site_tensors, mpo, left_in, right_in, tile_rows):
    chain = lax.axis_index("chain")
    sector = lax.axis_index("sector")
    sites, _, tile, _, _ = site_tensors.shape
    width = mpo.shape[1]
    padded = -(-width // 16) * 16
    pitch = tile + PITCH_EXTRA
    kept = masked(site_tensors[:, 0], tile_rows, chain * sites, sector, sector_count)
    am = kept.transpose(0, 2, 1, 3)
    at = kept.transpose(0, 2, 3, 1)
    extra = padded - width
    wide = jnp.pad(mpo, ((0, 0), (0, extra), (0, extra), (0, 0), (0, 0)))
    ml, mr = [], []
    for lo, hi in groups:
        part = wide[..., lo:hi, lo:hi]
        side = (hi - lo) * padded
        ml.append(part.transpose(0, 4, 2, 3, 1).reshape(sites, side, side))
        mr.append(part.transpose(0, 4, 1, 3, 2).reshape(sites, side, side))
    env = (width, tile, tile)
    sizes = (chain_count, sector_count, sites, width, tile, padded, pitch)
    vmem = pl.BlockSpec(memory_space=pltpu.VMEM)
    streams = 4 * sites + 1
    left, right, edge = pl.pallas_call(
        functools.partial(kernel, sizes),
        out_shape=(
            jax.ShapeDtypeStruct((sites,) + env, jnp.bfloat16),
            jax.ShapeDtypeStruct((sites,) + env, jnp.bfloat16),
            jax.ShapeDtypeStruct(env, jnp.bfloat16),
        ),
        in_specs=[vmem] * 10,
        out_specs=[vmem] * 3,
        scratch_shapes=[pltpu.VMEM((sites,) + env, jnp.bfloat16)] * 6
        + [
            pltpu.VMEM((2 * padded * pitch, tile), jnp.float32),
            pltpu.VMEM((padded * pitch, tile), jnp.float32),
            pltpu.VMEM((padded * pitch, tile), jnp.float32),
            pltpu.VMEM((padded * pitch, tile), jnp.float32),
            pltpu.SemaphoreType.DMA((streams, SLICES)),
            pltpu.SemaphoreType.DMA((streams, SLICES)),
        ],
        compiler_params=pltpu.CompilerParams(
            collective_id=0, has_side_effects=True, vmem_limit_bytes=67043328
        ),
    )(left_in[0, 0], right_in[0, 0], am, at, *ml, *mr)
    return left[:, None], right[:, None], edge[None, None]


def solution(mesh):
    envs = P("chain", "sector", None, None, None)
    return jax.shard_map(
        functools.partial(shards, mesh.shape["chain"], mesh.shape["sector"]),
        mesh=mesh,
        in_specs=(envs, P("chain", None, None, None, None), envs, envs, P()),
        out_specs=(envs, envs, envs),
        check_vma=False,
    )
```

profile of v0, /device:TPU:16, one launch (start us, length us, event | category | flops | bytes accessed | tf_op | source)
XLA Modules:
  0.0 177.5 jit_solution(2109118446989800580)
XLA Ops:
  0.6 0.8 pad_dynamic-slice_fusion
  1.4 0.1 slice_reduce_fusion
  1.5 0.1 iota_compare_fusion.1
  1.6 0.1 fusion.4
  1.7 0.1 pad_add_fusion
  1.8 0.1 iota_compare_fusion
  1.8 1.1 copy.15
  3.0 0.9 fusion
  3.9 0.8 copy.19.am
  4.7 1.1 copy.16
  5.8 0.0 copy-start.2
  5.8 0.0 copy-start.3
  5.9 0.1 copy.18
  6.0 0.7 reshape.56.mr1
  6.7 0.7 copy.20.ml0
  7.4 0.7 copy.21.ml2
  8.1 0.1 copy.17
  8.2 0.7 reshape.54.ml1
  9.0 161.2 %shard_map.76 = (bf16[2,42,128,128]{3,2,1,0:T(8,128)(2,1)}, bf16[2,42,128,128]{3,2,1,0:T(8,128)(2,1)}, bf16[42,128,128]{2,1,0:T(8,128)(2,1)}) custom-call(bf16[42,128,128]{2,1,0:T(8,128)(2,1)} %bitcast.33, bf16[42,128,128]{2,1,0:T(8,128)(2,1)} %bitcast.34, bf16[2,4,128,128]{3,2,1,0:T(8,128)(2,1)} %copy.19.am, bf16[2,4,128,128]{3,2,1,0:T(8,128)(2,1)} %get-tuple-element.19.at, ...), custom_call_target="tpu_custom_call" | custom-call | tf_op jit(solution)/shard_map/pallas_call | solution.py:276
  170.2 0.0 copy-start
  170.2 3.8 %copy.27 = bf16[2,1,42,128,128]{4,3,2,1,0:T(8,128)(2,1)} copy(bf16[2,1,42,128,128]{4,3,2,1,0:T(8,128)(2,1)} %bitcast.32) | data formatting | bytes 5505024
  174.0 1.5 copy.28
  175.6 0.8 copy-done.1
  176.4 1.1 copy.29
  (6 shorter events, 0.1 us)
Async XLA Ops:
  5.8 2.4 %copy-start.2 = (bf16[2,48,48,1,1]{2,1,0,4,3:T(8,128)(2,1)}, bf16[2,48,48,1,1]{2,1,0,4,3:T(8,128)(2,1)S(1)}, u32[]{:S(2)}) copy-start(bf16[2,48,48,1,1]{2,1,0,4,3:T(8,128)(2,1)S(1)} %get-tuple-element.17) | copy-start | bytes 27652
  5.8 2.4 %copy-start.3 = (bf16[2,48,48,1,1]{2,1,0,4,3:T(8,128)(2,1)}, bf16[2,48,48,1,1]{2,1,0,4,3:T(8,128)(2,1)S(1)}, u32[]{:S(2)}) copy-start(bf16[2,48,48,1,1]{2,1,0,4,3:T(8,128)(2,1)S(1)} %get-tuple-element.18) | copy-start | bytes 27652
  170.2 3.8 %copy-start = (bf16[2,42,128,128]{3,2,1,0:T(8,128)(2,1)S(1)}, bf16[2,42,128,128]{3,2,1,0:T(8,128)(2,1)}, u32[]{:S(2)}) copy-start(bf16[2,42,128,128]{3,2,1,0:T(8,128)(2,1)} %get-tuple-element.7) | copy-start | bytes 8257540
  174.0 2.3 %copy-start.1 = (bf16[42,128,128]{2,1,0:T(8,128)(2,1)S(1)}, bf16[42,128,128]{2,1,0:T(8,128)(2,1)}, u32[]{:S(2)}) copy-start(bf16[42,128,128]{2,1,0:T(8,128)(2,1)} %get-tuple-element.8) | copy-start | bytes 4128772
where the time goes:
time: 178 us; the launch traced here: 177 us
  Pallas kernels  161 us (90%)
  local copies, waits for them, and re-layouts  14.3 us (8%)
    pallas_call x1, Pallas kernels, shards(): pl.pallas_call(functools.partial(kernel, sizes), out_shape=(jax.ShapeDtyp...  161 us
    unnamed x13, local copies, waits for them, and re-layouts  9.44 us

commit v1 on v0

v1 whole, which is shorter than its diff:
```python
import functools

import jax
import jax.numpy as jnp
from jax import lax
from jax.experimental import pallas as pl
from jax.experimental.pallas import tpu as pltpu
from jax.sharding import PartitionSpec as P

groups = ((0, 1), (1, 3), (3, 4))
charge = (0, 1, 1, 2)
SLICES = 4
PITCH_EXTRA = 8
ROWS = 16
PAIRS = 3


def stage_one(width, tile, padded, pitch, src, lhs, mid):
    count = lhs.shape[0] // tile
    pairs = width // 2
    unroll = max(n for n in range(1, PAIRS + 1) if pairs % n == 0)

    def body(i, carry):
        for k in range(unroll):
            w = (i * unroll + k) * 2
            rhs = jnp.concatenate([src[w], src[w + 1]], axis=1)
            prod = jnp.dot(lhs, rhs, preferred_element_type=jnp.float32)
            for s in range(count):
                for j in range(2):
                    row = pl.multiple_of((s * padded + w + j) * pitch, 8)
                    mid[pl.ds(row, tile), :] = prod[
                        s * tile : (s + 1) * tile, j * tile : (j + 1) * tile
                    ]
        return carry

    lax.fori_loop(0, pairs // unroll, body, 0)


def stage_two(tile, padded, pitch, start, rows, mid, mpo_part, fin, out, add):
    count = fin.shape[0] // tile

    def block(i, carry):
        base = start + i * ROWS
        left = []
        for j in range(0, ROWS, 2):
            both = [
                mid[pl.ds(base + j + k, count * padded, stride=pitch), :].astype(
                    jnp.bfloat16
                )
                for k in range(2)
            ]
            inner = jnp.dot(
                mpo_part,
                jnp.concatenate(both, axis=1),
                preferred_element_type=jnp.float32,
            ).astype(jnp.bfloat16)
            for k in range(2):
                left.append(
                    jnp.concatenate(
                        [
                            inner[
                                t * padded : (t + 1) * padded,
                                k * tile : (k + 1) * tile,
                            ]
                            for t in range(count)
                        ],
                        axis=1,
                    )
                )
        prod = jnp.dot(
            jnp.concatenate(left, axis=0), fin, preferred_element_type=jnp.float32
        )
        for j in range(ROWS):
            spot = pl.ds(base + j, padded, stride=pitch)
            value = prod[j * padded : (j + 1) * padded]
            if add:
                value = value + out[spot, :]
            out[spot, :] = value
        return carry

    lax.fori_loop(0, rows // ROWS, block, 0)


def emit(width, pitch, start, rows, acc, other, dst):
    def one(i, carry):
        for k in range(2):
            w = 2 * i + k
            value = acc[pl.ds(pl.multiple_of(w * pitch + start, 8), rows), :]
            if other is not None:
                value = value + other[w, start : start + rows, :].astype(jnp.float32)
            dst[w, start : start + rows, :] = value.astype(jnp.bfloat16)
        return carry

    lax.fori_loop(0, width // 2, one, 0)


def kernel(
    sizes,
    rows_ref, a_in, m_in, lin_hbm, rin_hbm,
    left_out, right_out, edge_out,
    lin, rin, r_one, r_two, p_send, p_recv, s_send, s_recv,
    mid, acc_one, acc_zero, acc_right, am, at, m_one, m_two, a_wide, m_wide,
    send_sem, recv_sem, load_sem,
):
    chain_count, sector_count, sites, width, tile, padded, pitch = sizes
    chain = lax.axis_index("chain")
    sector = lax.axis_index("sector")
    up = lax.rem(sector + 1, sector_count)
    down = lax.rem(sector + sector_count - 1, sector_count)
    after = lax.rem(chain + 1, chain_count)
    before = lax.rem(chain + chain_count - 1, chain_count)
    rows = tile // SLICES

    barrier = pltpu.get_barrier_semaphore()
    for there in ({"sector": up}, {"sector": down}, {"chain": after}, {"chain": before}):
        pl.semaphore_signal(barrier, inc=1, device_id=there)
    load_left = pltpu.make_async_copy(lin_hbm, lin, load_sem.at[0])
    load_right = pltpu.make_async_copy(rin_hbm, rin, load_sem.at[1])
    load_left.start()
    load_right.start()

    def piece(src, dst, stream, c, there):
        cut = (slice(None), pl.ds(c * rows, rows), slice(None))
        return pltpu.make_async_remote_copy(
            src_ref=src.at[cut],
            dst_ref=dst.at[cut],
            send_sem=send_sem.at[stream, c],
            recv_sem=recv_sem.at[stream, c],
            device_id=there,
            device_id_type=pl.DeviceIdType.MESH,
        )

    ids_a = lax.broadcasted_iota(jnp.int32, (tile, tile), 0)
    ids_b = lax.broadcasted_iota(jnp.int32, (tile, tile), 1)

    def widen(site):
        a_wide[site] = a_in[site].astype(jnp.float32)
        m_wide[site, 0 : 16 * width, 0:width] = m_in[site].astype(jnp.float32)

    def prepare_tensor(site, t):
        bond = chain * sites + site
        there = sector + charge[t]
        seen = rows_ref[bond + 1, jnp.minimum(there, sector_count - 1)]
        high = jnp.where(there < sector_count, seen, 0)
        keep = (ids_a < rows_ref[bond, sector]) & (ids_b < high)
        value = jnp.where(keep, a_wide[site, pl.ds(t, tile, stride=4), :], 0.0)
        am[site, t] = value.astype(jnp.bfloat16)
        at[site, t] = value.T.astype(jnp.bfloat16)

    def corner(side, site, s, t):
        value = m_wide[site, pl.ds(4 * s + t, padded, stride=16), :]
        if side == 0:
            full = jnp.concatenate(
                [value, jnp.zeros((tile - padded, tile), jnp.float32)], axis=0
            )
            value = full.T[:padded]
        return value

    def prepare_mpo(side, site, n):
        lo, hi = groups[n]
        for t in range(lo, hi):
            value = corner(side, site, lo, t)
            for s in range(lo + 1, hi):
                value = value + pltpu.roll(
                    corner(side, site, s, t), (s - lo) * padded, 1
                )
            value = value.astype(jnp.bfloat16)
            if n == 1:
                m_two[side, site, (t - lo) * padded : (t - lo + 1) * padded] = value
            else:
                m_one[side, site, n // 2] = value

    def mpo_of(side, site, n):
        if n == 1:
            return m_two[side, site, :, : 2 * padded]
        return m_one[side, site, n // 2, :, :padded]

    def stack_of(mats, site, n):
        lo, hi = groups[n]
        return mats[site, lo:hi].reshape((hi - lo) * tile, tile)

    one = functools.partial(stage_one, width, tile, padded, pitch)
    two = functools.partial(stage_two, tile, padded, pitch)
    out = functools.partial(emit, width, pitch)

    def first(side, src, site, n):
        one(src, stack_of(am if side else at, site, n), mid)

    def second(side, site, n, start, count, acc, add):
        two(
            start, count, mid, mpo_of(side, site, n),
            stack_of(at if side else am, site, n), acc, add,
        )

    def both(side, src, site, n, acc, add):
        first(side, src, site, n)
        second(side, site, n, 0, tile, acc, add)

    m_wide[...] = jnp.zeros_like(m_wide)
    zero = jnp.zeros((tile, tile), jnp.float32)
    for s in range(2):
        for w in range(width, padded):
            mid[pl.ds((s * padded + w) * pitch, tile), :] = zero
    pl.semaphore_wait(barrier, 4)

    copies = []
    for c in range(SLICES):
        copies.append(piece(rin_hbm, r_one.at[0], 0, c, {"sector": down}))
        copies[-1].start()
    own = copies[-SLICES:]
    widen(0)
    prepare_tensor(0, 3)
    prepare_mpo(0, 0, 2)
    load_left.wait()
    left_src = lin
    right_src = rin
    for step in range(sites):
        base = step * 4
        lsite, rsite = step, sites - 1 - step
        first(0, left_src, lsite, 2)
        firsts = []
        own = own if step == 0 else []
        for c in range(SLICES):
            second(0, lsite, 2, c * rows, rows, acc_one, False)
            out(c * rows, rows, acc_one, None, p_send.at[step])
            firsts.append(
                piece(p_send.at[step], p_recv.at[step], base + 1, c, {"sector": up})
            )
            firsts[-1].start()
        if step > 0:
            first(1, r_two.at[step - 1], rsite + 1, 2)
            for c in range(SLICES):
                second(1, rsite + 1, 2, c * rows, rows, acc_right, True)
                out(c * rows, rows, acc_right, None, right_out.at[rsite + 1])
                own.append(
                    piece(
                        right_out.at[rsite + 1], r_one.at[step], base, c,
                        {"sector": down},
                    )
                )
                own[-1].start()
            copies += own
            right_src = right_out.at[rsite + 1]
        if step == 0:
            for t in range(3):
                prepare_tensor(0, t)
            for site in range(1, sites):
                widen(site)
                for t in range(4):
                    prepare_tensor(site, t)
            for side in range(2):
                for site in range(sites):
                    for n in range(3):
                        if (side, site, n) != (0, 0, 2):
                            prepare_mpo(side, site, n)
        both(0, left_src, lsite, 1, acc_one, False)
        if step == 0:
            load_right.wait()
        both(1, right_src, rsite, 0, acc_right, False)
        seconds, relays = [], []
        for c in range(SLICES):
            firsts[c].wait_recv()
            out(c * rows, rows, acc_one, p_recv.at[step], s_send.at[step])
            seconds.append(
                piece(s_send.at[step], s_recv.at[step], base + 2, c, {"sector": up})
            )
            seconds[-1].start()
            own[c].wait_recv()
            relays.append(
                piece(r_one.at[step], r_two.at[step], base + 3, c, {"sector": down})
            )
            relays[-1].start()
        both(0, left_src, lsite, 0, acc_zero, False)
        both(1, r_one.at[step], rsite, 1, acc_right, True)
        last = step == sites - 1
        for c in range(SLICES):
            seconds[c].wait_recv()
            out(c * rows, rows, acc_zero, s_recv.at[step], left_out.at[lsite])
            if last:
                edge = piece(left_out.at[lsite], edge_out, 4 * sites, c, {"chain": after})

                @pl.when(chain < chain_count - 1)
                def _(edge=edge):
                    edge.start()

        left_src = left_out.at[lsite]
        for c in range(SLICES):
            relays[c].wait_recv()
        copies += firsts + seconds + relays
    both(1, r_two.at[sites - 1], 0, 2, acc_right, True)
    for c in range(SLICES):
        out(c * rows, rows, acc_right, None, right_out.at[0])

    @pl.when(chain == 0)
    def _():
        def keep(w, carry):
            edge_out[w] = lin[w]
            return carry

        lax.fori_loop(0, width, keep, 0)

    for c in range(SLICES):
        edge = piece(left_out.at[sites - 1], edge_out, 4 * sites, c, {"chain": after})

        @pl.when(chain > 0)
        def _(edge=edge):
            edge.wait_recv()

        @pl.when(chain < chain_count - 1)
        def _(edge=edge):
            edge.wait_send()

    for copy in copies:
        copy.wait_send()


def shards(chain_count, sector_count, site_tensors, mpo, left_in, right_in, tile_rows):
    sites, _, tile, phys, _ = site_tensors.shape
    width = mpo.shape[1]
    padded = -(-width // 16) * 16
    pitch = tile + PITCH_EXTRA
    tensors = site_tensors.reshape(sites, tile * phys, tile)
    flat_mpo = mpo.transpose(0, 1, 3, 4, 2).reshape(sites, width * 16, width)
    env = (width, tile, tile)
    sizes = (chain_count, sector_count, sites, width, tile, padded, pitch)
    vmem = pl.BlockSpec(memory_space=pltpu.VMEM)
    hbm = pl.BlockSpec(memory_space=pl.ANY)
    streams = 4 * sites + 1
    left, right, edge = pl.pallas_call(
        functools.partial(kernel, sizes),
        out_shape=(
            pltpu.VMEM((sites,) + env, jnp.bfloat16),
            pltpu.VMEM((sites,) + env, jnp.bfloat16),
            pltpu.VMEM(env, jnp.bfloat16),
        ),
        in_specs=[pl.BlockSpec(memory_space=pltpu.SMEM), vmem, vmem, hbm, hbm],
        out_specs=[vmem] * 3,
        scratch_shapes=[pltpu.VMEM(env, jnp.bfloat16)] * 2
        + [pltpu.VMEM((sites,) + env, jnp.bfloat16)] * 6
        + [
            pltpu.VMEM((2 * padded * pitch, tile), jnp.float32),
            pltpu.VMEM((padded * pitch, tile), jnp.float32),
            pltpu.VMEM((padded * pitch, tile), jnp.float32),
            pltpu.VMEM((padded * pitch, tile), jnp.float32),
            pltpu.VMEM((sites, phys, tile, tile), jnp.bfloat16),
            pltpu.VMEM((sites, phys, tile, tile), jnp.bfloat16),
            pltpu.VMEM((2, sites, 2, padded, tile), jnp.bfloat16),
            pltpu.VMEM((2, sites, 2 * padded, tile), jnp.bfloat16),
            pltpu.VMEM((sites, phys * tile, tile), jnp.float32),
            pltpu.VMEM((sites, 16 * padded, tile), jnp.float32),
            pltpu.SemaphoreType.DMA((streams, SLICES)),
            pltpu.SemaphoreType.DMA((streams, SLICES)),
            pltpu.SemaphoreType.DMA((2,)),
        ],
        compiler_params=pltpu.CompilerParams(
            collective_id=0, has_side_effects=True, vmem_limit_bytes=52 << 20
        ),
    )(tile_rows, tensors, flat_mpo, left_in[0, 0], right_in[0, 0])
    return left[:, None], right[:, None], edge[None, None]


def solution(mesh):
    envs = P("chain", "sector", None, None, None)
    return jax.shard_map(
        functools.partial(shards, mesh.shape["chain"], mesh.shape["sector"]),
        mesh=mesh,
        in_specs=(envs, P("chain", None, None, None, None), envs, envs, P()),
        out_specs=(envs, envs, envs),
        check_vma=False,
    )
```

time: 178 us -> 149 us (0.84)
  Pallas kernels: 161 us -> 145 us
  local copies, waits for them, and re-layouts: 14.3 us -> 4.15 us
    pallas_call x1, Pallas kernels: 161 us -> 145 us  [shards(): pl.pallas_call(functools.partial(kernel, sizes), out_shape=(pltpu.VMEM((s...]
    unnamed x13 -> x3, local copies, waits for them, and re-layouts: 9.44 us -> 4.15 us
    reshape x4 -> x0, local copies, waits for them, and re-layouts: 2.82 us -> none  [the longest x3 2.1 us: shards(): ml.append(part.transpose(0, 4, 2, 3, 1).reshape(sites, side, side))]
where the time goes in v1:
time: 149 us
  Pallas kernels  145 us (97%)
  local copies, waits for them, and re-layouts  4.15 us (3%)
    pallas_call x1, Pallas kernels, shards(): pl.pallas_call(functools.partial(kernel, sizes), out_shape=(pltpu.VMEM((s...  145 us
    unnamed x3, local copies, waits for them, and re-layouts  4.15 us

profile of v1, /device:TPU:16, one launch (start us, length us, event | category | flops | bytes accessed | tf_op | source)
XLA Modules:
  0.0 149.3 jit_solution(17246814657449667942)
XLA Ops:
  0.6 144.5 %shard_map.76 = (bf16[2,42,128,128]{3,2,1,0:T(8,128)(2,1)S(1)}, bf16[2,42,128,128]{3,2,1,0:T(8,128)(2,1)S(1)}, bf16[42,128,128]{2,1,0:T(8,128)(2,1)S(1)}) custom-call(s32[17,32]{1,0:T(8,128)} %rows_ref.1, bf16[2,512,128]{2,1,0:T(8,128)(2,1)} %bitcast.19, bf16[2,672,42]{2,1,0:T(8,128)(2,1)} %bitcast.18, bf16[42,128,128]{2,1,0:T(8,128)(2,1)} %bitcast.16, ...), custom_call_target="tpu_custom_call" | custom-call | tf_op jit(solution)/shard_map/pallas_call | solution.py:329
  145.1 1.5 %copy.13 = bf16[2,1,42,128,128]{4,3,2,1,0:T(8,128)(2,1)} copy(bf16[2,1,42,128,128]{4,3,2,1,0:T(8,128)(2,1)S(1)} %bitcast.14) | data formatting | bytes 5505024
  146.7 1.5 %copy.14 = bf16[2,1,42,128,128]{4,3,2,1,0:T(8,128)(2,1)} copy(bf16[2,1,42,128,128]{4,3,2,1,0:T(8,128)(2,1)S(1)} %bitcast.13) | data formatting | bytes 5505024
  148.2 1.1 copy.15

commit v2 on v1

v2 whole, which is shorter than its diff:
```python
import functools

import jax
import jax.numpy as jnp
from jax import lax
from jax.experimental import pallas as pl
from jax.experimental.pallas import tpu as pltpu
from jax.sharding import PartitionSpec as P

groups = ((0, 1), (1, 3), (3, 4))
charge = (0, 1, 1, 2)
SLICES = 4
SPAN = 6
PITCH_EXTRA = 8
ROWS = 16
PAIRS = 3


def stage_one(tile, padded, pitch, start, width, src, lhs, mid):
    count = lhs.shape[0] // tile
    pairs = width // 2
    unroll = max(n for n in range(1, PAIRS + 1) if pairs % n == 0)

    def body(i, carry):
        for k in range(unroll):
            w = start + (i * unroll + k) * 2
            rhs = jnp.concatenate([src[w], src[w + 1]], axis=1)
            prod = jnp.dot(lhs, rhs, preferred_element_type=jnp.float32)
            for s in range(count):
                for j in range(2):
                    row = pl.multiple_of((s * padded + w + j) * pitch, 8)
                    mid[pl.ds(row, tile), :] = prod[
                        s * tile : (s + 1) * tile, j * tile : (j + 1) * tile
                    ]
        return carry

    lax.fori_loop(0, pairs // unroll, body, 0)


def stage_two(tile, padded, pitch, start, rows, mid, mpo_part, fin, out, add):
    count = fin.shape[0] // tile

    def block(i, carry):
        base = start + i * ROWS
        left = []
        for j in range(0, ROWS, 2):
            both = [
                mid[pl.ds(base + j + k, count * padded, stride=pitch), :].astype(
                    jnp.bfloat16
                )
                for k in range(2)
            ]
            inner = jnp.dot(
                mpo_part,
                jnp.concatenate(both, axis=1),
                preferred_element_type=jnp.float32,
            ).astype(jnp.bfloat16)
            for k in range(2):
                left.append(
                    jnp.concatenate(
                        [
                            inner[
                                t * padded : (t + 1) * padded,
                                k * tile : (k + 1) * tile,
                            ]
                            for t in range(count)
                        ],
                        axis=1,
                    )
                )
        prod = jnp.dot(
            jnp.concatenate(left, axis=0), fin, preferred_element_type=jnp.float32
        )
        for j in range(ROWS):
            spot = pl.ds(base + j, padded, stride=pitch)
            value = prod[j * padded : (j + 1) * padded]
            if add:
                value = value + out[spot, :]
            out[spot, :] = value
        return carry

    lax.fori_loop(0, rows // ROWS, block, 0)


def ket_first(width, padded, pitch, start, rows, src, fin, mpo_part, mid, inner):
    group = max(n for n in range(1, 7) if width % n == 0)

    def body(i, carry):
        first = i * group
        block = src[pl.ds(first, group), start : start + rows, :]
        prod = jnp.dot(
            block.reshape(group * rows, block.shape[2]),
            fin,
            preferred_element_type=jnp.float32,
        )
        for k in range(group):
            row = pl.multiple_of((first + k) * pitch + start, 8)
            mid[pl.ds(row, rows), :] = prod[k * rows : (k + 1) * rows]
        return carry

    lax.fori_loop(0, width // group, body, 0)
    tile = fin.shape[1]

    def block(i, carry):
        for j in range(0, ROWS, 2):
            base = start + i * ROWS + j
            both = [
                mid[pl.ds(base + k, padded, stride=pitch), :].astype(jnp.bfloat16)
                for k in range(2)
            ]
            prod = jnp.dot(
                mpo_part,
                jnp.concatenate(both, axis=1),
                preferred_element_type=jnp.float32,
            )
            for k in range(2):
                inner[pl.ds(base + k, padded, stride=pitch), :] = prod[
                    :, k * tile : (k + 1) * tile
                ]
        return carry

    lax.fori_loop(0, rows // ROWS, block, 0)


def bra_last(tile, pitch, start, width, inner, lhs, acc, dst):
    for w in range(start, start + width, 2):
        rows = [pl.ds((w + k) * pitch, tile) for k in range(2)]
        rhs = jnp.concatenate(
            [inner[row, :].astype(jnp.bfloat16) for row in rows], axis=1
        )
        prod = jnp.dot(lhs, rhs, preferred_element_type=jnp.float32)
        for k in range(2):
            value = prod[:, k * tile : (k + 1) * tile]
            if acc is not None:
                value = value + acc[rows[k], :]
            dst[w + k] = value.astype(jnp.bfloat16)


def emit(pitch, wide, tall, acc, other, dst):
    first, width = wide
    start, rows = tall

    def one(i, carry):
        for k in range(2):
            w = first + 2 * i + k
            value = acc[pl.ds(pl.multiple_of(w * pitch + start, 8), rows), :]
            if other is not None:
                value = value + other[w, start : start + rows, :].astype(jnp.float32)
            dst[w, start : start + rows, :] = value.astype(jnp.bfloat16)
        return carry

    lax.fori_loop(0, width // 2, one, 0)


def in_order(*lists):
    spots = []
    for at, (count, act) in enumerate(lists):
        spots += [((c + 1) / count, at, c, act) for c in range(count)]
    for _, _, c, act in sorted(spots, key=lambda spot: spot[:3]):
        act(c)


def kernel(
    sizes,
    rows_ref, a_hbm, m_hbm, lin_hbm, rin_hbm,
    left_out, right_out, edge_out,
    lin, rin, r_one, r_two, p_send, p_recv, s_send, s_recv,
    mid, mid_bra, mid_ket, inner, acc_one, acc_zero, acc_right,
    am, at, m_one, m_two, a_in, m_in, a_wide, m_wide,
    send_sem, recv_sem, load_sem,
):
    chain_count, sector_count, sites, width, tile, padded, pitch = sizes
    chain = lax.axis_index("chain")
    sector = lax.axis_index("sector")
    up = lax.rem(sector + 1, sector_count)
    down = lax.rem(sector + sector_count - 1, sector_count)
    after = lax.rem(chain + 1, chain_count)
    before = lax.rem(chain + chain_count - 1, chain_count)
    rows = tile // SLICES
    chunks = width // SPAN

    barrier = pltpu.get_barrier_semaphore()
    for there in ({"sector": up}, {"sector": down}, {"chain": after}, {"chain": before}):
        pl.semaphore_signal(barrier, inc=1, device_id=there)
    loads = [
        pltpu.make_async_copy(src, dst, load_sem.at[i])
        for i, (src, dst) in enumerate(
            ((a_hbm, a_in), (m_hbm, m_in), (lin_hbm, lin), (rin_hbm, rin))
        )
    ]
    for load in loads:
        load.start()
    keep_edge = pltpu.make_async_copy(lin_hbm, edge_out, load_sem.at[4])

    @pl.when(chain == 0)
    def _():
        keep_edge.start()

    def piece(form, src, dst, stream, c, there):
        if form == "bra":
            cut = (slice(None), pl.ds(c * rows, rows), slice(None))
        else:
            cut = (pl.ds(c * SPAN, SPAN), slice(None), slice(None))
        return pltpu.make_async_remote_copy(
            src_ref=src.at[cut],
            dst_ref=dst.at[cut],
            send_sem=send_sem.at[stream, c],
            recv_sem=recv_sem.at[stream, c],
            device_id=there,
            device_id_type=pl.DeviceIdType.MESH,
        )

    def pieces(form, src, dst, stream, there):
        count = SLICES if form == "bra" else chunks
        return [piece(form, src, dst, stream, c, there) for c in range(count)]

    ids_a = lax.broadcasted_iota(jnp.int32, (tile, tile), 0)
    ids_b = lax.broadcasted_iota(jnp.int32, (tile, tile), 1)

    def widen(site):
        a_wide[site] = a_in[site].astype(jnp.float32)
        m_wide[site, 0 : 16 * width, 0:width] = m_in[site].astype(jnp.float32)

    def prepare_tensor(site, t):
        bond = chain * sites + site
        there = sector + charge[t]
        seen = rows_ref[bond + 1, jnp.minimum(there, sector_count - 1)]
        high = jnp.where(there < sector_count, seen, 0)
        keep = (ids_a < rows_ref[bond, sector]) & (ids_b < high)
        value = jnp.where(keep, a_wide[site, pl.ds(t, tile, stride=4), :], 0.0)
        am[site, t] = value.astype(jnp.bfloat16)
        at[site, t] = value.T.astype(jnp.bfloat16)

    def corner(side, site, s, t):
        value = m_wide[site, pl.ds(4 * s + t, padded, stride=16), :]
        if side == 0:
            full = jnp.concatenate(
                [value, jnp.zeros((tile - padded, tile), jnp.float32)], axis=0
            )
            value = full.T[:padded]
        return value

    def prepare_mpo(side, site, n):
        lo, hi = groups[n]
        for t in range(lo, hi):
            value = corner(side, site, lo, t)
            for s in range(lo + 1, hi):
                value = value + pltpu.roll(
                    corner(side, site, s, t), (s - lo) * padded, 1
                )
            value = value.astype(jnp.bfloat16)
            if n == 1:
                m_two[side, site, (t - lo) * padded : (t - lo + 1) * padded] = value
            else:
                m_one[side, site, n // 2] = value

    def mpo_of(side, site, n):
        if n == 1:
            return m_two[side, site, :, : 2 * padded]
        return m_one[side, site, n // 2, :, :padded]

    def stack_of(mats, site, n):
        lo, hi = groups[n]
        return mats[site, lo:hi].reshape((hi - lo) * tile, tile)

    one = functools.partial(stage_one, tile, padded, pitch)
    two = functools.partial(stage_two, tile, padded, pitch)
    every = (0, width)
    whole = (0, tile)

    def tall(c):
        return (c * rows, rows)

    def wide(c):
        return (c * SPAN, SPAN)

    def first(side, src, site, n, part, dst):
        one(*part, src, stack_of(am if side else at, site, n), dst)

    def second(side, site, n, part, src, acc, add):
        two(
            *part, src, mpo_of(side, site, n),
            stack_of(at if side else am, site, n), acc, add,
        )

    def both(side, src, site, n, acc, add):
        first(side, src, site, n, every, mid)
        second(side, site, n, whole, mid, acc, add)

    def ket(side, src, site, part):
        ket_first(
            width, padded, pitch, *part, src, stack_of(at if side else am, site, 2),
            mpo_of(side, site, 2), mid_ket, inner,
        )

    def bra(side, site, part, acc, dst):
        bra_last(
            tile, pitch, *part, inner, stack_of(am if side else at, site, 2), acc, dst
        )

    zero = jnp.zeros((tile, tile), jnp.float32)
    for w in range(width, padded):
        for buffer, s in ((mid, 0), (mid, 1), (mid_bra, 0), (mid_ket, 0)):
            buffer[pl.ds((s * padded + w) * pitch, tile), :] = zero
    m_wide[...] = jnp.zeros_like(m_wide)
    loads[0].wait()
    loads[1].wait()
    widen(0)
    prepare_tensor(0, 3)
    prepare_mpo(0, 0, 2)
    loads[2].wait()
    first(0, lin, 0, 2, every, mid)
    pl.semaphore_wait(barrier, 4)
    r_own = pieces("bond", rin_hbm, r_one.at[0], 0, {"sector": down})
    for copy in r_own:
        copy.start()
    p_own = pieces("bra", p_send.at[0], p_recv.at[0], 1, {"sector": up})
    for c in range(SLICES):
        second(0, 0, 2, tall(c), mid, acc_one, False)
        emit(pitch, every, tall(c), acc_one, None, p_send.at[0])
        p_own[c].start()
    for t in range(3):
        prepare_tensor(0, t)
    widen(1)
    for t in range(4):
        prepare_tensor(1, t)
    for side in range(2):
        for site in range(sites):
            for n in range(3):
                if (side, site, n) != (0, 0, 2):
                    prepare_mpo(side, site, n)

    both(0, lin, 0, 1, acc_one, False)
    loads[3].wait()
    both(1, rin, 1, 0, acc_right, False)
    s_own = pieces("bra", s_send.at[0], s_recv.at[0], 2, {"sector": up})
    r_pass = pieces("bond", r_one.at[0], r_two.at[0], 3, {"sector": down})

    def on_partial(c):
        p_own[c].wait_recv()
        emit(pitch, every, tall(c), acc_one, p_recv.at[0], s_send.at[0])
        s_own[c].start()

    def on_right(c):
        r_own[c].wait_recv()
        r_pass[c].start()

    in_order((chunks, on_right), (SLICES, on_partial))
    both(0, lin, 0, 0, acc_zero, False)
    both(1, r_one.at[0], 1, 1, acc_right, True)

    def on_sum(c):
        s_own[c].wait_recv()
        emit(pitch, every, tall(c), acc_zero, s_recv.at[0], left_out.at[0])
        ket(0, left_out.at[0], 1, tall(c))

    def on_second_right(c):
        r_pass[c].wait_recv()
        first(1, r_two.at[0], 1, 2, wide(c), mid_bra)

    in_order((chunks, on_second_right), (SLICES, on_sum))
    copies = r_own + p_own + s_own + r_pass

    p_own = pieces("bond", p_send.at[1], p_recv.at[1], 5, {"sector": up})
    r_own = pieces("bra", right_out.at[1], r_one.at[1], 4, {"sector": down})

    def send_partial(c):
        bra(0, 1, wide(c), None, p_send.at[1])
        p_own[c].start()

    def send_right(c):
        second(1, 1, 2, tall(c), mid_bra, acc_right, True)
        emit(pitch, every, tall(c), acc_right, None, right_out.at[1])
        r_own[c].start()

    in_order((chunks, send_partial), (SLICES, send_right))

    both(0, left_out.at[0], 1, 1, acc_one, False)
    both(1, right_out.at[1], 0, 0, acc_right, False)
    s_own = pieces("bond", s_send.at[1], s_recv.at[1], 6, {"sector": up})
    r_pass = pieces("bra", r_one.at[1], r_two.at[1], 7, {"sector": down})
    edges = pieces("bond", left_out.at[1], edge_out, 8, {"chain": after})

    def on_partial(c):
        p_own[c].wait_recv()
        emit(pitch, wide(c), whole, acc_one, p_recv.at[1], s_send.at[1])
        s_own[c].start()

    def on_right(c):
        r_own[c].wait_recv()
        r_pass[c].start()

    in_order((SLICES, on_right), (chunks, on_partial))
    both(0, left_out.at[0], 1, 0, acc_zero, False)
    both(1, r_one.at[1], 0, 1, acc_right, True)

    def on_sum(c):
        s_own[c].wait_recv()
        emit(pitch, wide(c), whole, acc_zero, s_recv.at[1], left_out.at[1])

        @pl.when(chain < chain_count - 1)
        def _():
            edges[c].start()

    def on_second_right(c):
        r_pass[c].wait_recv()
        ket(1, r_two.at[1], 0, tall(c))

    in_order((chunks, on_sum), (SLICES, on_second_right))
    bra(1, 0, every, acc_right, right_out.at[0])
    copies += r_own + p_own + s_own + r_pass

    @pl.when(chain == 0)
    def _():
        keep_edge.wait()

    @pl.when(chain > 0)
    def _():
        for edge in edges:
            edge.wait_recv()

    @pl.when(chain < chain_count - 1)
    def _():
        for edge in edges:
            edge.wait_send()

    for copy in copies:
        copy.wait_send()


def shards(chain_count, sector_count, site_tensors, mpo, left_in, right_in, tile_rows):
    sites, _, tile, phys, _ = site_tensors.shape
    width = mpo.shape[1]
    padded = -(-width // 16) * 16
    pitch = tile + PITCH_EXTRA
    tensors = site_tensors.reshape(sites, tile * phys, tile)
    flat_mpo = mpo.transpose(0, 1, 3, 4, 2).reshape(sites, width * 16, width)
    env = (width, tile, tile)
    sizes = (chain_count, sector_count, sites, width, tile, padded, pitch)
    vmem = pl.BlockSpec(memory_space=pltpu.VMEM)
    hbm = pl.BlockSpec(memory_space=pl.ANY)
    streams = 4 * sites + 1
    most = max(SLICES, width // SPAN)
    left, right, edge = pl.pallas_call(
        functools.partial(kernel, sizes),
        out_shape=(
            pltpu.VMEM((sites,) + env, jnp.bfloat16),
            pltpu.VMEM((sites,) + env, jnp.bfloat16),
            pltpu.VMEM(env, jnp.bfloat16),
        ),
        in_specs=[pl.BlockSpec(memory_space=pltpu.SMEM)] + [hbm] * 4,
        out_specs=[vmem] * 3,
        scratch_shapes=[pltpu.VMEM(env, jnp.bfloat16)] * 2
        + [pltpu.VMEM((sites,) + env, jnp.bfloat16)] * 6
        + [
            pltpu.VMEM((2 * padded * pitch, tile), jnp.float32),
        ]
        + [pltpu.VMEM((padded * pitch, tile), jnp.float32)] * 6
        + [
            pltpu.VMEM((sites, phys, tile, tile), jnp.bfloat16),
            pltpu.VMEM((sites, phys, tile, tile), jnp.bfloat16),
            pltpu.VMEM((2, sites, 2, padded, tile), jnp.bfloat16),
            pltpu.VMEM((2, sites, 2 * padded, tile), jnp.bfloat16),
            pltpu.VMEM((sites, phys * tile, tile), jnp.bfloat16),
            pltpu.VMEM((sites, 16 * width, width), jnp.bfloat16),
            pltpu.VMEM((sites, phys * tile, tile), jnp.float32),
            pltpu.VMEM((sites, 16 * padded, tile), jnp.float32),
            pltpu.SemaphoreType.DMA((streams, most)),
            pltpu.SemaphoreType.DMA((streams, most)),
            pltpu.SemaphoreType.DMA((5,)),
        ],
        compiler_params=pltpu.CompilerParams(
            collective_id=0, has_side_effects=True, vmem_limit_bytes=52 << 20
        ),
    )(tile_rows, tensors, flat_mpo, left_in[0, 0], right_in[0, 0])
    return left[:, None], right[:, None], edge[None, None]


def solution(mesh):
    envs = P("chain", "sector", None, None, None)
    return jax.shard_map(
        functools.partial(shards, mesh.shape["chain"], mesh.shape["sector"]),
        mesh=mesh,
        in_specs=(envs, P("chain", None, None, None, None), envs, envs, P()),
        out_specs=(envs, envs, envs),
        check_vma=False,
    )
```

time: 149 us -> 143 us (0.960)
  Pallas kernels: 145 us -> 138 us
    pallas_call x1, Pallas kernels: 145 us -> 138 us  [shards(): pl.pallas_call(functools.partial(kernel, sizes), out_shape=(pltpu.VMEM((s...]
where the time goes in v2:
time: 143 us
  Pallas kernels  138 us (97%)
  local copies, waits for them, and re-layouts  4.15 us (3%)
    pallas_call x1, Pallas kernels, shards(): pl.pallas_call(functools.partial(kernel, sizes), out_shape=(pltpu.VMEM((s...  138 us
    unnamed x3, local copies, waits for them, and re-layouts  4.15 us

profile of v2, /device:TPU:16, one launch (start us, length us, event | category | flops | bytes accessed | tf_op | source)
XLA Modules:
  0.0 142.8 jit_solution(12990017066352231656)
XLA Ops:
  0.6 138.0 %shard_map.76 = (bf16[2,42,128,128]{3,2,1,0:T(8,128)(2,1)S(1)}, bf16[2,42,128,128]{3,2,1,0:T(8,128)(2,1)S(1)}, bf16[42,128,128]{2,1,0:T(8,128)(2,1)S(1)}) custom-call(s32[17,32]{1,0:T(8,128)} %rows_ref.1, bf16[2,512,128]{2,1,0:T(8,128)(2,1)} %bitcast.19, bf16[2,672,42]{2,1,0:T(8,128)(2,1)} %bitcast.18, bf16[42,128,128]{2,1,0:T(8,128)(2,1)} %bitcast.16, ...), custom_call_target="tpu_custom_call" | custom-call | tf_op jit(solution)/shard_map/pallas_call | solution.py:444
  138.7 1.5 %copy.13 = bf16[2,1,42,128,128]{4,3,2,1,0:T(8,128)(2,1)} copy(bf16[2,1,42,128,128]{4,3,2,1,0:T(8,128)(2,1)S(1)} %bitcast.14) | data formatting | bytes 5505024
  140.2 1.5 %copy.14 = bf16[2,1,42,128,128]{4,3,2,1,0:T(8,128)(2,1)} copy(bf16[2,1,42,128,128]{4,3,2,1,0:T(8,128)(2,1)S(1)} %bitcast.13) | data formatting | bytes 5505024
  141.7 1.1 copy.15

commit v3 on v2

--- a/solution.py
+++ b/solution.py
@@ -9,8 +9,9 @@
 
 groups = ((0, 1), (1, 3), (3, 4))
 charge = (0, 1, 1, 2)
-SLICES = 4
+SLICES = 8
 SPAN = 6
+ENDS = (4, 2)
 PITCH_EXTRA = 8
 ROWS = 16
 PAIRS = 3
@@ -83,7 +84,7 @@
 
 
 def ket_first(width, padded, pitch, start, rows, src, fin, mpo_part, mid, inner):
-    group = max(n for n in range(1, 7) if width % n == 0)
+    group = max(n for n in range(1, 22) if width % n == 0)
 
     def body(i, carry):
         first = i * group
@@ -152,6 +153,13 @@
     lax.fori_loop(0, width // 2, one, 0)
 
 
+def chunks_of(width):
+    spans = [SPAN] * ((width - sum(ENDS)) // SPAN)
+    spans += [width - sum(ENDS) - sum(spans)] + list(ENDS)
+    spans = [span for span in spans if span]
+    return [(sum(spans[:i]), span) for i, span in enumerate(spans)]
+
+
 def in_order(*lists):
     spots = []
     for at, (count, act) in enumerate(lists):
@@ -162,11 +170,11 @@
 
 def kernel(
     sizes,
-    rows_ref, a_hbm, m_hbm, lin_hbm, rin_hbm,
+    rows_hbm, a_hbm, m_hbm, lin_hbm, rin_hbm,
     left_out, right_out, edge_out,
     lin, rin, r_one, r_two, p_send, p_recv, s_send, s_recv,
     mid, mid_bra, mid_ket, inner, acc_one, acc_zero, acc_right,
-    am, at, m_one, m_two, a_in, m_in, a_wide, m_wide,
+    am, at, m_one, m_two, a_in, m_in, a_wide, m_wide, rows_ref,
     send_sem, recv_sem, load_sem,
 ):
     chain_count, sector_count, sites, width, tile, padded, pitch = sizes
@@ -177,7 +185,9 @@
     after = lax.rem(chain + 1, chain_count)
     before = lax.rem(chain + chain_count - 1, chain_count)
     rows = tile // SLICES
-    chunks = width // SPAN
+    parts = chunks_of(width)
+    chunks = len(parts)
+    even = lax.rem(chain, 2) == 0
 
     barrier = pltpu.get_barrier_semaphore()
     for there in ({"sector": up}, {"sector": down}, {"chain": after}, {"chain": before}):
@@ -185,12 +195,12 @@
     loads = [
         pltpu.make_async_copy(src, dst, load_sem.at[i])
         for i, (src, dst) in enumerate(
-            ((a_hbm, a_in), (m_hbm, m_in), (lin_hbm, lin), (rin_hbm, rin))
+            ((rows_hbm, rows_ref), (a_hbm, a_in), (m_hbm, m_in), (lin_hbm, lin), (rin_hbm, rin))
         )
     ]
     for load in loads:
         load.start()
-    keep_edge = pltpu.make_async_copy(lin_hbm, edge_out, load_sem.at[4])
+    keep_edge = pltpu.make_async_copy(lin_hbm, edge_out, load_sem.at[5])
 
     @pl.when(chain == 0)
     def _():
@@ -200,7 +210,7 @@
         if form == "bra":
             cut = (slice(None), pl.ds(c * rows, rows), slice(None))
         else:
-            cut = (pl.ds(c * SPAN, SPAN), slice(None), slice(None))
+            cut = (pl.ds(*parts[c]), slice(None), slice(None))
         return pltpu.make_async_remote_copy(
             src_ref=src.at[cut],
             dst_ref=dst.at[cut],
@@ -272,7 +282,7 @@
         return (c * rows, rows)
 
     def wide(c):
-        return (c * SPAN, SPAN)
+        return parts[c]
 
     def first(side, src, site, n, part, dst):
         one(*part, src, stack_of(am if side else at, site, n), dst)
@@ -298,27 +308,31 @@
             tile, pitch, *part, inner, stack_of(am if side else at, site, 2), acc, dst
         )
 
+    m_wide[...] = jnp.zeros_like(m_wide)
     zero = jnp.zeros((tile, tile), jnp.float32)
     for w in range(width, padded):
         for buffer, s in ((mid, 0), (mid, 1), (mid_bra, 0), (mid_ket, 0)):
             buffer[pl.ds((s * padded + w) * pitch, tile), :] = zero
-    m_wide[...] = jnp.zeros_like(m_wide)
-    loads[0].wait()
-    loads[1].wait()
+    for i in range(3):
+        loads[i].wait()
     widen(0)
     prepare_tensor(0, 3)
     prepare_mpo(0, 0, 2)
-    loads[2].wait()
+    loads[3].wait()
     first(0, lin, 0, 2, every, mid)
     pl.semaphore_wait(barrier, 4)
     r_own = pieces("bond", rin_hbm, r_one.at[0], 0, {"sector": down})
-    for copy in r_own:
-        copy.start()
     p_own = pieces("bra", p_send.at[0], p_recv.at[0], 1, {"sector": up})
+
+    @pl.when(even)
+    def _():
+        for copy in r_own:
+            copy.start()
+
     for c in range(SLICES):
         second(0, 0, 2, tall(c), mid, acc_one, False)
         emit(pitch, every, tall(c), acc_one, None, p_send.at[0])
-        p_own[c].start()
+        pl.when(even)(p_own[c].start)
     for t in range(3):
         prepare_tensor(0, t)
     widen(1)
@@ -331,8 +345,14 @@
                     prepare_mpo(side, site, n)
 
     both(0, lin, 0, 1, acc_one, False)
-    loads[3].wait()
+    loads[4].wait()
     both(1, rin, 1, 0, acc_right, False)
+
+    @pl.when(jnp.logical_not(even))
+    def _():
+        for copy in r_own + p_own:
+            copy.start()
+
     s_own = pieces("bra", s_send.at[0], s_recv.at[0], 2, {"sector": up})
     r_pass = pieces("bond", r_one.at[0], r_two.at[0], 3, {"sector": down})
 
@@ -392,7 +412,6 @@
 
     in_order((SLICES, on_right), (chunks, on_partial))
     both(0, left_out.at[0], 1, 0, acc_zero, False)
-    both(1, r_one.at[1], 0, 1, acc_right, True)
 
     def on_sum(c):
         s_own[c].wait_recv()
@@ -406,7 +425,17 @@
         r_pass[c].wait_recv()
         ket(1, r_two.at[1], 0, tall(c))
 
-    in_order((chunks, on_sum), (SLICES, on_second_right))
+    on_sum(0)
+    on_sum(1)
+    first(1, r_one.at[1], 0, 1, every, mid)
+    on_sum(2)
+    quarters = [(i * tile // 4, tile // 4) for i in range(4)]
+    for i in range(2):
+        second(1, 0, 1, quarters[i], mid, acc_right, True)
+    on_sum(3)
+    for i in range(2, 4):
+        second(1, 0, 1, quarters[i], mid, acc_right, True)
+    in_order((chunks - 4, lambda c: on_sum(c + 4)), (SLICES, on_second_right))
     bra(1, 0, every, acc_right, right_out.at[0])
     copies += r_own + p_own + s_own + r_pass
 
@@ -426,6 +455,37 @@
 
     for copy in copies:
         copy.wait_send()
+
+
+def leave(left, right, edge):
+    def body(left, right, edge, left_out, right_out, edge_out, sem):
+        pairs = [(edge, edge_out.at[0, 0])]
+        for src, dst in ((left, left_out), (right, right_out)):
+            pairs += [(src.at[i], dst.at[i, 0]) for i in range(src.shape[0])]
+        copies = [
+            pltpu.make_async_copy(src, dst, sem.at[i])
+            for i, (src, dst) in enumerate(pairs)
+        ]
+        for copy in copies:
+            copy.start()
+        for copy in copies:
+            copy.wait()
+
+    env = edge.shape
+    sites = left.shape[0]
+    hbm = pl.BlockSpec(memory_space=pl.ANY)
+    return pl.pallas_call(
+        body,
+        out_shape=(
+            jax.ShapeDtypeStruct((sites, 1) + env, left.dtype),
+            jax.ShapeDtypeStruct((sites, 1) + env, left.dtype),
+            jax.ShapeDtypeStruct((1, 1) + env, left.dtype),
+        ),
+        in_specs=[pl.BlockSpec(memory_space=pltpu.VMEM)] * 3,
+        out_specs=[hbm] * 3,
+        scratch_shapes=[pltpu.SemaphoreType.DMA((2 * sites + 1,))],
+        compiler_params=pltpu.CompilerParams(vmem_limit_bytes=16 << 20),
+    )(left, right, edge)
 
 
 def shards(chain_count, sector_count, site_tensors, mpo, left_in, right_in, tile_rows):
@@ -440,7 +500,7 @@
     vmem = pl.BlockSpec(memory_space=pltpu.VMEM)
     hbm = pl.BlockSpec(memory_space=pl.ANY)
     streams = 4 * sites + 1
-    most = max(SLICES, width // SPAN)
+    most = max(SLICES, len(chunks_of(width)))
     left, right, edge = pl.pallas_call(
         functools.partial(kernel, sizes),
         out_shape=(
@@ -448,7 +508,7 @@
             pltpu.VMEM((sites,) + env, jnp.bfloat16),
             pltpu.VMEM(env, jnp.bfloat16),
         ),
-        in_specs=[pl.BlockSpec(memory_space=pltpu.SMEM)] + [hbm] * 4,
+        in_specs=[hbm] * 5,
         out_specs=[vmem] * 3,
         scratch_shapes=[pltpu.VMEM(env, jnp.bfloat16)] * 2
         + [pltpu.VMEM((sites,) + env, jnp.bfloat16)] * 6
@@ -465,15 +525,16 @@
             pltpu.VMEM((sites, 16 * width, width), jnp.bfloat16),
             pltpu.VMEM((sites, phys * tile, tile), jnp.float32),
             pltpu.VMEM((sites, 16 * padded, tile), jnp.float32),
+            pltpu.SMEM(tile_rows.shape, tile_rows.dtype),
             pltpu.SemaphoreType.DMA((streams, most)),
             pltpu.SemaphoreType.DMA((streams, most)),
-            pltpu.SemaphoreType.DMA((5,)),
+            pltpu.SemaphoreType.DMA((6,)),
         ],
         compiler_params=pltpu.CompilerParams(
             collective_id=0, has_side_effects=True, vmem_limit_bytes=52 << 20
         ),
     )(tile_rows, tensors, flat_mpo, left_in[0, 0], right_in[0, 0])
-    return left[:, None], right[:, None], edge[None, None]
+    return leave(left, right, edge)
 
 
 def solution(mesh):

time: 143 us -> 140 us (0.979)
  local copies, waits for them, and re-layouts: 4.15 us -> 0 us
    unnamed x3 -> x0, local copies, waits for them, and re-layouts: 4.15 us -> none
    pallas_call x0 -> x1, Pallas kernels: none -> 2.93 us  [leave(): pl.pallas_call(body, out_shape=(jax.ShapeDtypeStruct((sites, 1) + env, le...]
    pallas_call x1, Pallas kernels: 138 us -> 136 us  [shards(): pl.pallas_call(functools.partial(kernel, sizes), out_shape=(pltpu.VMEM((s...]
where the time goes in v3:
time: 140 us
  Pallas kernels  139 us (99%)
    pallas_call x1, Pallas kernels, shards(): pl.pallas_call(functools.partial(kernel, sizes), out_shape=(pltpu.VMEM((s...  136 us
    pallas_call x1, Pallas kernels, leave(): pl.pallas_call(body, out_shape=(jax.ShapeDtypeStruct((sites, 1) + env, le...  2.93 us

profile of v3, /device:TPU:16, one launch (start us, length us, event | category | flops | bytes accessed | tf_op | source)
XLA Modules:
  0.0 139.9 jit_solution(6239087549017665534)
XLA Ops:
  0.6 136.2 %shard_map.76 = (bf16[2,42,128,128]{3,2,1,0:T(8,128)(2,1)S(1)}, bf16[2,42,128,128]{3,2,1,0:T(8,128)(2,1)S(1)}, bf16[42,128,128]{2,1,0:T(8,128)(2,1)S(1)}) custom-call(s32[17,32]{1,0:T(8,128)} %rows_hbm.1, bf16[2,512,128]{2,1,0:T(8,128)(2,1)} %bitcast.9, bf16[2,672,42]{2,1,0:T(8,128)(2,1)} %bitcast.8, bf16[42,128,128]{2,1,0:T(8,128)(2,1)} %bitcast.6, ...), custom_call_target="tpu_custom_call" | custom-call | tf_op jit(solution)/shard_map/pallas_call | solution.py:504
  136.8 2.9 %shard_map.77 = (bf16[2,1,42,128,128]{4,3,2,1,0:T(8,128)(2,1)}, bf16[2,1,42,128,128]{4,3,2,1,0:T(8,128)(2,1)}, bf16[1,1,42,128,128]{4,3,2,1,0:T(8,128)(2,1)}) custom-call(bf16[2,42,128,128]{3,2,1,0:T(8,128)(2,1)S(1)} %get-tuple-element.6.left, bf16[2,42,128,128]{3,2,1,0:T(8,128)(2,1)S(1)} %get-tuple-element.7.right, ...), custom_call_target="tpu_custom_call" | custom-call | tf_op jit(solution)/shard_map/pallas_call | solution.py:477

commit v4 on v3

--- a/solution.py
+++ b/solution.py
@@ -11,8 +11,9 @@
 charge = (0, 1, 1, 2)
 SLICES = 8
 SPAN = 6
-ENDS = (4, 2)
+ENDS = (2, 4)
 PITCH_EXTRA = 8
+PARTS = 3
 ROWS = 16
 PAIRS = 3
 
@@ -154,18 +155,48 @@
 
 
 def chunks_of(width):
-    spans = [SPAN] * ((width - sum(ENDS)) // SPAN)
-    spans += [width - sum(ENDS) - sum(spans)] + list(ENDS)
+    middle = width - 2 * sum(ENDS)
+    spans = list(ENDS) + [SPAN] * (middle // SPAN) + [middle % SPAN] + list(ENDS[::-1])
     spans = [span for span in spans if span]
     return [(sum(spans[:i]), span) for i, span in enumerate(spans)]
 
 
 def in_order(*lists):
     spots = []
-    for at, (count, act) in enumerate(lists):
-        spots += [((c + 1) / count, at, c, act) for c in range(count)]
+    for at, (ends, act) in enumerate(lists):
+        spots += [(end, at, c, act) for c, end in enumerate(ends)]
     for _, _, c, act in sorted(spots, key=lambda spot: spot[:3]):
         act(c)
+
+
+class Stream:
+    def __init__(self, copies, send, receive):
+        self.copies, self.send, self.receive = copies, send, receive
+
+    def start(self, c, also=None):
+        send = self.send if also is None else jnp.logical_and(self.send, also)
+        pl.when(send)(self.copies[c].start)
+
+    def start_all(self, also):
+        @pl.when(jnp.logical_and(self.send, also))
+        def _():
+            for copy in self.copies:
+                copy.start()
+
+    def wait_recv(self, c):
+        pl.when(self.receive)(self.copies[c].wait_recv)
+
+    def wait_all(self):
+        @pl.when(self.receive)
+        def _():
+            for copy in self.copies:
+                copy.wait_recv()
+
+    def finish(self):
+        @pl.when(self.send)
+        def _():
+            for copy in self.copies:
+                copy.wait_send()
 
 
 def kernel(
@@ -187,11 +218,26 @@
     rows = tile // SLICES
     parts = chunks_of(width)
     chunks = len(parts)
-    even = lax.rem(chain, 2) == 0
+    ahead = lax.rem(chain, 2) == 1
+    bra_ends = [(c + 1) / SLICES for c in range(SLICES)]
+    bond_ends = [sum(part) / width for part in parts]
+    above, below = sector < sector_count - 1, sector > 0
+    later, earlier = chain < chain_count - 1, chain > 0
 
     barrier = pltpu.get_barrier_semaphore()
-    for there in ({"sector": up}, {"sector": down}, {"chain": after}, {"chain": before}):
-        pl.semaphore_signal(barrier, inc=1, device_id=there)
+    greeted = jnp.int32(0)
+    for known, there in (
+        (above, {"sector": up}),
+        (below, {"sector": down}),
+        (later, {"chain": after}),
+        (earlier, {"chain": before}),
+    ):
+
+        @pl.when(known)
+        def _(there=there):
+            pl.semaphore_signal(barrier, inc=1, device_id=there)
+
+        greeted = greeted + jnp.where(known, 1, 0)
     loads = [
         pltpu.make_async_copy(src, dst, load_sem.at[i])
         for i, (src, dst) in enumerate(
@@ -222,7 +268,14 @@
 
     def pieces(form, src, dst, stream, there):
         count = SLICES if form == "bra" else chunks
-        return [piece(form, src, dst, stream, c, there) for c in range(count)]
+        copies = [piece(form, src, dst, stream, c, there) for c in range(count)]
+        send, receive = {
+            0: (below, above),
+            1: (above, below),
+            2: (above, below),
+            3: (below & above, sector < sector_count - 2),
+        }[stream % 4]
+        return Stream(copies, send, receive)
 
     ids_a = lax.broadcasted_iota(jnp.int32, (tile, tile), 0)
     ids_b = lax.broadcasted_iota(jnp.int32, (tile, tile), 1)
@@ -313,6 +366,10 @@
     for w in range(width, padded):
         for buffer, s in ((mid, 0), (mid, 1), (mid_bra, 0), (mid_ket, 0)):
             buffer[pl.ds((s * padded + w) * pitch, tile), :] = zero
+    r_own = pieces("bond", rin_hbm, r_one.at[0], 0, {"sector": down})
+    p_own = pieces("bra", p_send.at[0], p_recv.at[0], 1, {"sector": up})
+    pl.semaphore_wait(barrier, greeted)
+    r_own.start_all(ahead)
     for i in range(3):
         loads[i].wait()
     widen(0)
@@ -320,19 +377,32 @@
     prepare_mpo(0, 0, 2)
     loads[3].wait()
     first(0, lin, 0, 2, every, mid)
-    pl.semaphore_wait(barrier, 4)
-    r_own = pieces("bond", rin_hbm, r_one.at[0], 0, {"sector": down})
-    p_own = pieces("bra", p_send.at[0], p_recv.at[0], 1, {"sector": up})
-
-    @pl.when(even)
-    def _():
-        for copy in r_own:
-            copy.start()
-
     for c in range(SLICES):
         second(0, 0, 2, tall(c), mid, acc_one, False)
         emit(pitch, every, tall(c), acc_one, None, p_send.at[0])
-        pl.when(even)(p_own[c].start)
+        p_own.start(c, ahead)
+
+    def clear(*buffers):
+        def body(w, carry):
+            for buffer in buffers:
+                for step in range(2):
+                    buffer[step, w] = jnp.zeros((tile, tile), jnp.bfloat16)
+            return carry
+
+        lax.fori_loop(0, width, body, 0)
+
+    @pl.when(jnp.logical_not(below))
+    def _():
+        clear(p_recv, s_recv)
+
+    @pl.when(jnp.logical_not(above))
+    def _():
+        clear(r_one)
+
+    @pl.when(sector >= sector_count - 2)
+    def _():
+        clear(r_two)
+
     for t in range(3):
         prepare_tensor(0, t)
     widen(1)
@@ -348,113 +418,110 @@
     loads[4].wait()
     both(1, rin, 1, 0, acc_right, False)
 
-    @pl.when(jnp.logical_not(even))
-    def _():
-        for copy in r_own + p_own:
-            copy.start()
-
+    r_own.start_all(jnp.logical_not(ahead))
+    p_own.start_all(jnp.logical_not(ahead))
     s_own = pieces("bra", s_send.at[0], s_recv.at[0], 2, {"sector": up})
     r_pass = pieces("bond", r_one.at[0], r_two.at[0], 3, {"sector": down})
 
     def on_partial(c):
-        p_own[c].wait_recv()
+        p_own.wait_recv(c)
         emit(pitch, every, tall(c), acc_one, p_recv.at[0], s_send.at[0])
-        s_own[c].start()
+        s_own.start(c)
 
     def on_right(c):
-        r_own[c].wait_recv()
-        r_pass[c].start()
-
-    in_order((chunks, on_right), (SLICES, on_partial))
+        r_own.wait_recv(c)
+        r_pass.start(c)
+
+    in_order((bond_ends, on_right), (bra_ends, on_partial))
     both(0, lin, 0, 0, acc_zero, False)
     both(1, r_one.at[0], 1, 1, acc_right, True)
 
     def on_sum(c):
-        s_own[c].wait_recv()
+        s_own.wait_recv(c)
         emit(pitch, every, tall(c), acc_zero, s_recv.at[0], left_out.at[0])
         ket(0, left_out.at[0], 1, tall(c))
 
     def on_second_right(c):
-        r_pass[c].wait_recv()
+        r_pass.wait_recv(c)
         first(1, r_two.at[0], 1, 2, wide(c), mid_bra)
 
-    in_order((chunks, on_second_right), (SLICES, on_sum))
-    copies = r_own + p_own + s_own + r_pass
+    in_order((bond_ends, on_second_right), (bra_ends, on_sum))
+    streams = [r_own, p_own, s_own, r_pass]
 
     p_own = pieces("bond", p_send.at[1], p_recv.at[1], 5, {"sector": up})
     r_own = pieces("bra", right_out.at[1], r_one.at[1], 4, {"sector": down})
 
     def send_partial(c):
         bra(0, 1, wide(c), None, p_send.at[1])
-        p_own[c].start()
+        p_own.start(c)
 
     def send_right(c):
         second(1, 1, 2, tall(c), mid_bra, acc_right, True)
         emit(pitch, every, tall(c), acc_right, None, right_out.at[1])
-        r_own[c].start()
-
-    in_order((chunks, send_partial), (SLICES, send_right))
+        r_own.start(c)
+
+    in_order((bond_ends, send_partial), (bra_ends, send_right))
 
     both(0, left_out.at[0], 1, 1, acc_one, False)
     both(1, right_out.at[1], 0, 0, acc_right, False)
     s_own = pieces("bond", s_send.at[1], s_recv.at[1], 6, {"sector": up})
     r_pass = pieces("bra", r_one.at[1], r_two.at[1], 7, {"sector": down})
-    edges = pieces("bond", left_out.at[1], edge_out, 8, {"chain": after})
+    edges = Stream(
+        [
+            piece("bond", left_out.at[1], edge_out, 8, c, {"chain": after})
+            for c in range(chunks)
+        ],
+        later,
+        earlier,
+    )
 
     def on_partial(c):
-        p_own[c].wait_recv()
+        p_own.wait_recv(c)
         emit(pitch, wide(c), whole, acc_one, p_recv.at[1], s_send.at[1])
-        s_own[c].start()
+        s_own.start(c)
 
     def on_right(c):
-        r_own[c].wait_recv()
-        r_pass[c].start()
-
-    in_order((SLICES, on_right), (chunks, on_partial))
+        r_own.wait_recv(c)
+        r_pass.start(c)
+
+    in_order((bra_ends, on_right), (bond_ends, on_partial))
     both(0, left_out.at[0], 1, 0, acc_zero, False)
 
     def on_sum(c):
-        s_own[c].wait_recv()
+        s_own.wait_recv(c)
         emit(pitch, wide(c), whole, acc_zero, s_recv.at[1], left_out.at[1])
 
-        @pl.when(chain < chain_count - 1)
-        def _():
-            edges[c].start()
+        edges.start(c)
 
     def on_second_right(c):
-        r_pass[c].wait_recv()
+        r_pass.wait_recv(c)
         ket(1, r_two.at[1], 0, tall(c))
 
     on_sum(0)
     on_sum(1)
+    on_sum(2)
     first(1, r_one.at[1], 0, 1, every, mid)
-    on_sum(2)
+    on_sum(3)
     quarters = [(i * tile // 4, tile // 4) for i in range(4)]
     for i in range(2):
         second(1, 0, 1, quarters[i], mid, acc_right, True)
-    on_sum(3)
+    on_sum(4)
     for i in range(2, 4):
         second(1, 0, 1, quarters[i], mid, acc_right, True)
-    in_order((chunks - 4, lambda c: on_sum(c + 4)), (SLICES, on_second_right))
+    done = bond_ends[4]
+    ends = [(end - done) / (1 - done) for end in bond_ends[5:]]
+    in_order((ends, lambda c: on_sum(c + 5)), (bra_ends, on_second_right))
     bra(1, 0, every, acc_right, right_out.at[0])
-    copies += r_own + p_own + s_own + r_pass
+    streams += [r_own, p_own, s_own, r_pass]
 
     @pl.when(chain == 0)
     def _():
         keep_edge.wait()
 
-    @pl.when(chain > 0)
-    def _():
-        for edge in edges:
-            edge.wait_recv()
-
-    @pl.when(chain < chain_count - 1)
-    def _():
-        for edge in edges:
-            edge.wait_send()
-
-    for copy in copies:
-        copy.wait_send()
+    edges.wait_all()
+    edges.finish()
+    for stream in streams:
+        stream.finish()
 
 
 def leave(left, right, edge):
@@ -462,6 +529,9 @@
         pairs = [(edge, edge_out.at[0, 0])]
         for src, dst in ((left, left_out), (right, right_out)):
             pairs += [(src.at[i], dst.at[i, 0]) for i in range(src.shape[0])]
+        third = edge.shape[0] // PARTS
+        cuts = [pl.ds(i * third, third) for i in range(PARTS)]
+        pairs = [(src.at[cut], dst.at[cut]) for src, dst in pairs for cut in cuts]
         copies = [
             pltpu.make_async_copy(src, dst, sem.at[i])
             for i, (src, dst) in enumerate(pairs)
@@ -483,7 +553,7 @@
         ),
         in_specs=[pl.BlockSpec(memory_space=pltpu.VMEM)] * 3,
         out_specs=[hbm] * 3,
-        scratch_shapes=[pltpu.SemaphoreType.DMA((2 * sites + 1,))],
+        scratch_shapes=[pltpu.SemaphoreType.DMA((PARTS * (2 * sites + 1),))],
         compiler_params=pltpu.CompilerParams(vmem_limit_bytes=16 << 20),
     )(left, right, edge)
 

time: 140 us -> 136 us (0.971)
  the two profiles are of different devices: /device:TPU:16 before, /device:TPU:7 now
where the time goes in v4:
time: 136 us
  Pallas kernels  135 us (99%)
    pallas_call x1, Pallas kernels, shards(): pl.pallas_call(functools.partial(kernel, sizes), out_shape=(pltpu.VMEM((s...  132 us
    pallas_call x1, Pallas kernels, leave(): pl.pallas_call(body, out_shape=(jax.ShapeDtypeStruct((sites, 1) + env, le...  2.96 us

profile of v4, /device:TPU:7, one launch (start us, length us, event | category | flops | bytes accessed | tf_op | source)
XLA Modules:
  0.0 135.6 jit_solution(4187402685263562057)
XLA Ops:
  0.6 131.9 %shard_map.76 = (bf16[2,42,128,128]{3,2,1,0:T(8,128)(2,1)S(1)}, bf16[2,42,128,128]{3,2,1,0:T(8,128)(2,1)S(1)}, bf16[42,128,128]{2,1,0:T(8,128)(2,1)S(1)}) custom-call(s32[17,32]{1,0:T(8,128)} %rows_hbm.1, bf16[2,512,128]{2,1,0:T(8,128)(2,1)} %bitcast.9, bf16[2,672,42]{2,1,0:T(8,128)(2,1)} %bitcast.8, bf16[42,128,128]{2,1,0:T(8,128)(2,1)} %bitcast.6, ...), custom_call_target="tpu_custom_call" | custom-call | tf_op jit(solution)/shard_map/pallas_call | solution.py:574
  132.5 3.0 %shard_map.77 = (bf16[2,1,42,128,128]{4,3,2,1,0:T(8,128)(2,1)}, bf16[2,1,42,128,128]{4,3,2,1,0:T(8,128)(2,1)}, bf16[1,1,42,128,128]{4,3,2,1,0:T(8,128)(2,1)}) custom-call(bf16[2,42,128,128]{3,2,1,0:T(8,128)(2,1)S(1)} %get-tuple-element.6.left, bf16[2,42,128,128]{3,2,1,0:T(8,128)(2,1)S(1)} %get-tuple-element.7.right, ...), custom_call_target="tpu_custom_call" | custom-call | tf_op jit(solution)/shard_map/pallas_call | solution.py:547

commit v5 on v4

--- a/solution.py
+++ b/solution.py
@@ -13,7 +13,8 @@
 SPAN = 6
 ENDS = (2, 4)
 PITCH_EXTRA = 8
-PARTS = 3
+LEAD = 0.9
+PARTS = 1
 ROWS = 16
 PAIRS = 3
 
@@ -85,7 +86,7 @@
 
 
 def ket_first(width, padded, pitch, start, rows, src, fin, mpo_part, mid, inner):
-    group = max(n for n in range(1, 22) if width % n == 0)
+    group = max(n for n in range(1, 43) if width % n == 0)
 
     def body(i, carry):
         first = i * group
@@ -170,8 +171,9 @@
 
 
 class Stream:
-    def __init__(self, copies, send, receive):
-        self.copies, self.send, self.receive = copies, send, receive
+    def __init__(self, copies, total, send, receive):
+        self.copies, self.total = copies, total
+        self.send, self.receive = send, receive
 
     def start(self, c, also=None):
         send = self.send if also is None else jnp.logical_and(self.send, also)
@@ -193,10 +195,7 @@
                 copy.wait_recv()
 
     def finish(self):
-        @pl.when(self.send)
-        def _():
-            for copy in self.copies:
-                copy.wait_send()
+        pl.when(self.send)(self.total.wait_send)
 
 
 def kernel(
@@ -252,7 +251,22 @@
     def _():
         keep_edge.start()
 
-    def piece(form, src, dst, stream, c, there):
+    forms = ("bond", "bra", "bra", "bond", "bra", "bond", "bond", "bra", "bond")
+    counts = {"bond": chunks, "bra": SLICES}
+    starts = [sum(counts[form] for form in forms[:i]) for i in range(len(forms))]
+
+    def total(src, dst, stream, there):
+        return pltpu.make_async_remote_copy(
+            src_ref=src,
+            dst_ref=dst,
+            send_sem=send_sem.at[stream],
+            recv_sem=recv_sem.at[starts[stream]],
+            device_id=there,
+            device_id_type=pl.DeviceIdType.MESH,
+        )
+
+    def piece(src, dst, stream, c, there):
+        form = forms[stream]
         if form == "bra":
             cut = (slice(None), pl.ds(c * rows, rows), slice(None))
         else:
@@ -260,22 +274,23 @@
         return pltpu.make_async_remote_copy(
             src_ref=src.at[cut],
             dst_ref=dst.at[cut],
-            send_sem=send_sem.at[stream, c],
-            recv_sem=recv_sem.at[stream, c],
+            send_sem=send_sem.at[stream],
+            recv_sem=recv_sem.at[starts[stream] + c],
             device_id=there,
             device_id_type=pl.DeviceIdType.MESH,
         )
 
-    def pieces(form, src, dst, stream, there):
-        count = SLICES if form == "bra" else chunks
-        copies = [piece(form, src, dst, stream, c, there) for c in range(count)]
-        send, receive = {
-            0: (below, above),
-            1: (above, below),
-            2: (above, below),
-            3: (below & above, sector < sector_count - 2),
-        }[stream % 4]
-        return Stream(copies, send, receive)
+    def pieces(src, dst, stream, there):
+        count = counts[forms[stream]]
+        copies = [piece(src, dst, stream, c, there) for c in range(count)]
+        send, receive = (
+            (below, above),
+            (above, below),
+            (above, below),
+            (below & above, sector < sector_count - 2),
+            (later, earlier),
+        )[stream % 4 if stream < 8 else 4]
+        return Stream(copies, total(src, dst, stream, there), send, receive)
 
     ids_a = lax.broadcasted_iota(jnp.int32, (tile, tile), 0)
     ids_b = lax.broadcasted_iota(jnp.int32, (tile, tile), 1)
@@ -366,17 +381,19 @@
     for w in range(width, padded):
         for buffer, s in ((mid, 0), (mid, 1), (mid_bra, 0), (mid_ket, 0)):
             buffer[pl.ds((s * padded + w) * pitch, tile), :] = zero
-    r_own = pieces("bond", rin_hbm, r_one.at[0], 0, {"sector": down})
-    p_own = pieces("bra", p_send.at[0], p_recv.at[0], 1, {"sector": up})
-    pl.semaphore_wait(barrier, greeted)
-    r_own.start_all(ahead)
+    r_own = pieces(rin_hbm, r_one.at[0], 0, {"sector": down})
+    p_own = pieces(p_send.at[0], p_recv.at[0], 1, {"sector": up})
     for i in range(3):
         loads[i].wait()
     widen(0)
     prepare_tensor(0, 3)
     prepare_mpo(0, 0, 2)
     loads[3].wait()
-    first(0, lin, 0, 2, every, mid)
+    most = width // (4 * PAIRS) * 2 * PAIRS
+    first(0, lin, 0, 2, (0, most), mid)
+    pl.semaphore_wait(barrier, greeted)
+    r_own.start_all(ahead)
+    first(0, lin, 0, 2, (most, width - most), mid)
     for c in range(SLICES):
         second(0, 0, 2, tall(c), mid, acc_one, False)
         emit(pitch, every, tall(c), acc_one, None, p_send.at[0])
@@ -420,8 +437,8 @@
 
     r_own.start_all(jnp.logical_not(ahead))
     p_own.start_all(jnp.logical_not(ahead))
-    s_own = pieces("bra", s_send.at[0], s_recv.at[0], 2, {"sector": up})
-    r_pass = pieces("bond", r_one.at[0], r_two.at[0], 3, {"sector": down})
+    s_own = pieces(s_send.at[0], s_recv.at[0], 2, {"sector": up})
+    r_pass = pieces(r_one.at[0], r_two.at[0], 3, {"sector": down})
 
     def on_partial(c):
         p_own.wait_recv(c)
@@ -446,10 +463,12 @@
         first(1, r_two.at[0], 1, 2, wide(c), mid_bra)
 
     in_order((bond_ends, on_second_right), (bra_ends, on_sum))
-    streams = [r_own, p_own, s_own, r_pass]
-
-    p_own = pieces("bond", p_send.at[1], p_recv.at[1], 5, {"sector": up})
-    r_own = pieces("bra", right_out.at[1], r_one.at[1], 4, {"sector": down})
+    for stream in (r_own, p_own):
+        stream.finish()
+    early = (s_own, r_pass)
+
+    p_own = pieces(p_send.at[1], p_recv.at[1], 5, {"sector": up})
+    r_own = pieces(right_out.at[1], r_one.at[1], 4, {"sector": down})
 
     def send_partial(c):
         bra(0, 1, wide(c), None, p_send.at[1])
@@ -464,16 +483,9 @@
 
     both(0, left_out.at[0], 1, 1, acc_one, False)
     both(1, right_out.at[1], 0, 0, acc_right, False)
-    s_own = pieces("bond", s_send.at[1], s_recv.at[1], 6, {"sector": up})
-    r_pass = pieces("bra", r_one.at[1], r_two.at[1], 7, {"sector": down})
-    edges = Stream(
-        [
-            piece("bond", left_out.at[1], edge_out, 8, c, {"chain": after})
-            for c in range(chunks)
-        ],
-        later,
-        earlier,
-    )
+    s_own = pieces(s_send.at[1], s_recv.at[1], 6, {"sector": up})
+    r_pass = pieces(r_one.at[1], r_two.at[1], 7, {"sector": down})
+    edges = pieces(left_out.at[1], edge_out, 8, {"chain": after})
 
     def on_partial(c):
         p_own.wait_recv(c)
@@ -497,6 +509,8 @@
         r_pass.wait_recv(c)
         ket(1, r_two.at[1], 0, tall(c))
 
+    for stream in early + (r_own, p_own):
+        stream.finish()
     on_sum(0)
     on_sum(1)
     on_sum(2)
@@ -510,9 +524,15 @@
         second(1, 0, 1, quarters[i], mid, acc_right, True)
     done = bond_ends[4]
     ends = [(end - done) / (1 - done) for end in bond_ends[5:]]
-    in_order((ends, lambda c: on_sum(c + 5)), (bra_ends, on_second_right))
-    bra(1, 0, every, acc_right, right_out.at[0])
-    streams += [r_own, p_own, s_own, r_pass]
+
+    def on_last_right(c):
+        if c < SLICES:
+            on_second_right(c)
+        else:
+            bra(1, 0, every, acc_right, right_out.at[0])
+
+    lead = [LEAD * end for end in bra_ends] + [LEAD]
+    in_order((lead, on_last_right), (ends, lambda c: on_sum(c + 5)))
 
     @pl.when(chain == 0)
     def _():
@@ -520,7 +540,7 @@
 
     edges.wait_all()
     edges.finish()
-    for stream in streams:
+    for stream in (s_own, r_pass):
         stream.finish()
 
 
@@ -569,8 +589,6 @@
     sizes = (chain_count, sector_count, sites, width, tile, padded, pitch)
     vmem = pl.BlockSpec(memory_space=pltpu.VMEM)
     hbm = pl.BlockSpec(memory_space=pl.ANY)
-    streams = 4 * sites + 1
-    most = max(SLICES, len(chunks_of(width)))
     left, right, edge = pl.pallas_call(
         functools.partial(kernel, sizes),
         out_shape=(
@@ -596,8 +614,8 @@
             pltpu.VMEM((sites, phys * tile, tile), jnp.float32),
             pltpu.VMEM((sites, 16 * padded, tile), jnp.float32),
             pltpu.SMEM(tile_rows.shape, tile_rows.dtype),
-            pltpu.SemaphoreType.DMA((streams, most)),
-            pltpu.SemaphoreType.DMA((streams, most)),
+            pltpu.SemaphoreType.DMA((9,)),
+            pltpu.SemaphoreType.DMA((4 * SLICES + 5 * len(chunks_of(width)),)),
             pltpu.SemaphoreType.DMA((6,)),
         ],
         compiler_params=pltpu.CompilerParams(

time: 136 us -> 135 us (level)
  the two profiles are of different devices: /device:TPU:7 before, /device:TPU:23 now
where the time goes in v5:
time: 135 us
  Pallas kernels  134 us (99%)
    pallas_call x1, Pallas kernels, shards(): pl.pallas_call(functools.partial(kernel, sizes), out_shape=(pltpu.VMEM((s...  131 us
    pallas_call x1, Pallas kernels, leave(): pl.pallas_call(body, out_shape=(jax.ShapeDtypeStruct((sites, 1) + env, le...  2.93 us

profile of v5, /device:TPU:23, one launch (start us, length us, event | category | flops | bytes accessed | tf_op | source)
XLA Modules:
  0.0 134.7 jit_solution(16086364403984042892)
XLA Ops:
  0.6 131.0 %shard_map.76 = (bf16[2,42,128,128]{3,2,1,0:T(8,128)(2,1)S(1)}, bf16[2,42,128,128]{3,2,1,0:T(8,128)(2,1)S(1)}, bf16[42,128,128]{2,1,0:T(8,128)(2,1)S(1)}) custom-call(s32[17,32]{1,0:T(8,128)} %rows_hbm.1, bf16[2,512,128]{2,1,0:T(8,128)(2,1)} %bitcast.9, bf16[2,672,42]{2,1,0:T(8,128)(2,1)} %bitcast.8, bf16[42,128,128]{2,1,0:T(8,128)(2,1)} %bitcast.6, ...), custom_call_target="tpu_custom_call" | custom-call | tf_op jit(solution)/shard_map/pallas_call | solution.py:592
  131.6 2.9 %shard_map.77 = (bf16[2,1,42,128,128]{4,3,2,1,0:T(8,128)(2,1)}, bf16[2,1,42,128,128]{4,3,2,1,0:T(8,128)(2,1)}, bf16[1,1,42,128,128]{4,3,2,1,0:T(8,128)(2,1)}) custom-call(bf16[2,42,128,128]{3,2,1,0:T(8,128)(2,1)S(1)} %get-tuple-element.6.left, bf16[2,42,128,128]{3,2,1,0:T(8,128)(2,1)S(1)} %get-tuple-element.7.right, ...), custom_call_target="tpu_custom_call" | custom-call | tf_op jit(solution)/shard_map/pallas_call | solution.py:567

commit v6 on v5

--- a/solution.py
+++ b/solution.py
@@ -240,16 +240,12 @@
     loads = [
         pltpu.make_async_copy(src, dst, load_sem.at[i])
         for i, (src, dst) in enumerate(
-            ((rows_hbm, rows_ref), (a_hbm, a_in), (m_hbm, m_in), (lin_hbm, lin), (rin_hbm, rin))
+            ((rows_hbm, rows_ref), (a_hbm, a_in), (lin_hbm, lin), (m_hbm, m_in), (rin_hbm, rin))
         )
     ]
-    for load in loads:
+    for load in loads[:4]:
         load.start()
     keep_edge = pltpu.make_async_copy(lin_hbm, edge_out, load_sem.at[5])
-
-    @pl.when(chain == 0)
-    def _():
-        keep_edge.start()
 
     forms = ("bond", "bra", "bra", "bond", "bra", "bond", "bond", "bra", "bond")
     counts = {"bond": chunks, "bra": SLICES}
@@ -295,8 +291,10 @@
     ids_a = lax.broadcasted_iota(jnp.int32, (tile, tile), 0)
     ids_b = lax.broadcasted_iota(jnp.int32, (tile, tile), 1)
 
-    def widen(site):
+    def widen_tensor(site):
         a_wide[site] = a_in[site].astype(jnp.float32)
+
+    def widen_mpo(site):
         m_wide[site, 0 : 16 * width, 0:width] = m_in[site].astype(jnp.float32)
 
     def prepare_tensor(site, t):
@@ -383,17 +381,25 @@
             buffer[pl.ds((s * padded + w) * pitch, tile), :] = zero
     r_own = pieces(rin_hbm, r_one.at[0], 0, {"sector": down})
     p_own = pieces(p_send.at[0], p_recv.at[0], 1, {"sector": up})
-    for i in range(3):
+    for i in range(2):
         loads[i].wait()
-    widen(0)
+    widen_tensor(0)
     prepare_tensor(0, 3)
-    prepare_mpo(0, 0, 2)
-    loads[3].wait()
+    loads[2].wait()
     most = width // (4 * PAIRS) * 2 * PAIRS
     first(0, lin, 0, 2, (0, most), mid)
     pl.semaphore_wait(barrier, greeted)
     r_own.start_all(ahead)
     first(0, lin, 0, 2, (most, width - most), mid)
+    loads[3].wait()
+    loads[4].start()
+
+    @pl.when(chain == 0)
+    def _():
+        keep_edge.start()
+
+    widen_mpo(0)
+    prepare_mpo(0, 0, 2)
     for c in range(SLICES):
         second(0, 0, 2, tall(c), mid, acc_one, False)
         emit(pitch, every, tall(c), acc_one, None, p_send.at[0])
@@ -422,7 +428,8 @@
 
     for t in range(3):
         prepare_tensor(0, t)
-    widen(1)
+    widen_tensor(1)
+    widen_mpo(1)
     for t in range(4):
         prepare_tensor(1, t)
     for side in range(2):

time: 135 us -> 135 us (level)
  the two profiles are of different devices: /device:TPU:23 before, /device:TPU:15 now
where the time goes in v6:
time: 135 us
  Pallas kernels  134 us (99%)
    pallas_call x1, Pallas kernels, shards(): pl.pallas_call(functools.partial(kernel, sizes), out_shape=(pltpu.VMEM((s...  131 us
    pallas_call x1, Pallas kernels, leave(): pl.pallas_call(body, out_shape=(jax.ShapeDtypeStruct((sites, 1) + env, le...  2.93 us

profile of v6, /device:TPU:15, one launch (start us, length us, event | category | flops | bytes accessed | tf_op | source)
XLA Modules:
  0.0 134.7 jit_solution(10399079576314877837)
XLA Ops:
  0.6 130.9 %shard_map.76 = (bf16[2,42,128,128]{3,2,1,0:T(8,128)(2,1)S(1)}, bf16[2,42,128,128]{3,2,1,0:T(8,128)(2,1)S(1)}, bf16[42,128,128]{2,1,0:T(8,128)(2,1)S(1)}) custom-call(s32[17,32]{1,0:T(8,128)} %rows_hbm.1, bf16[2,512,128]{2,1,0:T(8,128)(2,1)} %bitcast.9, bf16[2,672,42]{2,1,0:T(8,128)(2,1)} %bitcast.8, bf16[42,128,128]{2,1,0:T(8,128)(2,1)} %bitcast.6, ...), custom_call_target="tpu_custom_call" | custom-call | tf_op jit(solution)/shard_map/pallas_call | solution.py:599
  131.6 2.9 %shard_map.77 = (bf16[2,1,42,128,128]{4,3,2,1,0:T(8,128)(2,1)}, bf16[2,1,42,128,128]{4,3,2,1,0:T(8,128)(2,1)}, bf16[1,1,42,128,128]{4,3,2,1,0:T(8,128)(2,1)}) custom-call(bf16[2,42,128,128]{3,2,1,0:T(8,128)(2,1)S(1)} %get-tuple-element.6.left, bf16[2,42,128,128]{3,2,1,0:T(8,128)(2,1)S(1)} %get-tuple-element.7.right, ...), custom_call_target="tpu_custom_call" | custom-call | tf_op jit(solution)/shard_map/pallas_call | solution.py:574
